TPU v7x, 32 devices: a whole 2x2x4 slice. The times are simulated.
32 devices in a mesh: groups: 2 (over y), inst: 4 (over z), space: 4 (over x, core).
Axes of the slice: x: 2, y: 2, z: 4, core: 2. Of those that a mesh axis runs over, the one named last changes fastest.
Arguments:
- flow_state: float32 [8, 5, 16, 16, 128], P(('groups', 'inst'), None, 'space'), parts along dimension 0, may hold values from -1 to 1
- period_match: int32 [16], replicated, may hold values from 0 to 15, each once
Outputs:
- residual: float32 [8, 5, 16, 16, 128], P(('groups', 'inst'), None, 'space'), parts along dimension 0
There are 2 independent parts, one for each index of `groups`. A program takes and returns all parts, laid end to end along the dimension named above; an argument that names none is the same for every part. Nothing has to cross between parts.
Inputs may be any that keep to these rules, and one draw needn't show every extreme that they name: period_match is a permutation of the 16 spanwise layers.
All inputs are finite; a program needn't handle non-finite values.
Results may differ from a plain program's by a relative error of at most 0.0003.
Values sent between devices are 32-bit elements; how exact they have to be, the bound alone decides.
No kernel may reach another device: no remote copies, remote signals or barrier semaphores. Data moves between devices by JAX's collectives and lax.ppermute only.
A program may use at most 64 MiB of HBM per device.

v0:
```python
import math
import jax
import jax.numpy as jnp
from jax import lax
from jax.sharding import PartitionSpec as P

gamma_gas = 1.4
prandtl = 0.72
viscosity = 0.1
pseudo_step = 0.03
entropy_share = 0.1


def from_behind(block, axis, distance):
    devices = range(lax.axis_size(axis))
    route = [((i - distance) % len(devices), i) for i in devices]
    return lax.ppermute(block, axis, route)


def extended(cells, sides, width):
    for axis, dim in sides:
        count = lax.axis_size(axis)
        ends = count - 1
        head = lax.slice_in_dim(cells, 0, width, axis=dim)
        tail = lax.slice_in_dim(cells, cells.shape[dim] - width, cells.shape[dim], axis=dim)
        cells = jnp.concatenate(
            [
                lax.ppermute(tail, axis, [(i, (i + 1) % count) for i in range(ends)]),
                cells,
                lax.ppermute(head, axis, [((i + 1) % count, i) for i in range(ends)]),
            ],
            axis=dim,
        )
    return cells


def from_draw(draws):
    shape = (5,) + (1,) * (draws.ndim - 1)
    offsets = jnp.array([1.0, 0.8, 0.0, 0.0, 0.8], jnp.float32).reshape(shape)
    spreads = jnp.array([0.3, 0.3, 0.3, 0.3, 0.2], jnp.float32).reshape(shape)
    return offsets + spreads * draws


def conserved(primitives):
    dens = primitives[0]
    velocity = primitives[1:4]
    kinetic = 0.5 * dens * jnp.sum(velocity * velocity, axis=0)
    energy = primitives[4] / (gamma_gas - 1.0) + kinetic
    return jnp.concatenate([dens[None], dens[None] * velocity, energy[None]], axis=0)


def primitive(conserved_vars):
    dens = conserved_vars[0]
    velocity = conserved_vars[1:4] / dens
    pressure = (gamma_gas - 1.0) * (
        conserved_vars[4] - 0.5 * dens * jnp.sum(velocity * velocity, axis=0)
    )
    return jnp.concatenate([dens[None], velocity, pressure[None]], axis=0)


def entropy_fix(eigen_val, sound_speed):
    spread = entropy_share * sound_speed
    magnitude = jnp.abs(eigen_val)
    return jnp.where(
        magnitude >= spread, magnitude, (eigen_val * eigen_val + spread * spread) / (2.0 * spread)
    )


def euler_flux(dens, velocity, pressure, enthalpy, normal):
    normal_vel = velocity[normal]
    values = [dens * normal_vel]
    for component in range(3):
        moment = dens * velocity[component] * normal_vel
        if component == normal:
            moment = moment + pressure
        values.append(moment)
    values.append(dens * enthalpy * normal_vel)
    return values


def face_flux(left_cells, right_cells, normal):
    dens_left, vel_left, pres_left = (left_cells[0], left_cells[1:4], left_cells[4])
    dens_right, vel_right, pres_right = (right_cells[0], right_cells[1:4], right_cells[4])
    ratio = gamma_gas / (gamma_gas - 1.0)
    sq_left = jnp.sum(vel_left * vel_left, axis=0)
    sq_right = jnp.sum(vel_right * vel_right, axis=0)
    enth_left = ratio * pres_left / dens_left + 0.5 * sq_left
    enth_right = ratio * pres_right / dens_right + 0.5 * sq_right
    flux_left = euler_flux(dens_left, vel_left, pres_left, enth_left, normal)
    flux_right = euler_flux(dens_right, vel_right, pres_right, enth_right, normal)
    root_left = jnp.sqrt(dens_left)
    root_right = jnp.sqrt(dens_right)
    root_sum = root_left + root_right
    vel_roe = (root_left * vel_left + root_right * vel_right) / root_sum
    enth_roe = (root_left * enth_left + root_right * enth_right) / root_sum
    speed_sq = jnp.sum(vel_roe * vel_roe, axis=0)
    sound_sq = (gamma_gas - 1.0) * (enth_roe - 0.5 * speed_sq)
    sound_speed = jnp.sqrt(sound_sq)
    normal_vel = vel_roe[normal]
    dens_roe = root_left * root_right
    jump_dens = dens_right - dens_left
    jump_pres = pres_right - pres_left
    jump_vel = vel_right - vel_left
    jump_normal = jump_vel[normal]
    wave_slow = (jump_pres - dens_roe * sound_speed * jump_normal) / (2.0 * sound_sq)
    wave_fast = (jump_pres + dens_roe * sound_speed * jump_normal) / (2.0 * sound_sq)
    wave_mid = jump_dens - jump_pres / sound_sq
    eigen_mid = entropy_fix(normal_vel, sound_speed)
    flux_slow = entropy_fix(normal_vel - sound_speed, sound_speed) * wave_slow
    flux_fast = entropy_fix(normal_vel + sound_speed, sound_speed) * wave_fast
    dissipation = [flux_slow + eigen_mid * wave_mid + flux_fast]
    for component in range(3):
        unit_dir = 1.0 if component == normal else 0.0
        term = flux_slow * (vel_roe[component] - unit_dir * sound_speed)
        term = term + eigen_mid * (
            wave_mid * vel_roe[component]
            + dens_roe * (jump_vel[component] - unit_dir * jump_normal)
        )
        term = term + flux_fast * (vel_roe[component] + unit_dir * sound_speed)
        dissipation.append(term)
    shear_work = jnp.sum(vel_roe * jump_vel, axis=0) - normal_vel * jump_normal
    energy_term = flux_slow * (enth_roe - normal_vel * sound_speed)
    energy_term = energy_term + eigen_mid * (wave_mid * 0.5 * speed_sq + dens_roe * shear_work)
    energy_term = energy_term + flux_fast * (enth_roe + normal_vel * sound_speed)
    dissipation.append(energy_term)
    jump_temp = pres_right / dens_right - pres_left / dens_left
    jump_kin = 0.5 * (sq_right - sq_left)
    viscous_terms = [
        jnp.zeros_like(jump_dens),
        jump_vel[0],
        jump_vel[1],
        jump_vel[2],
        jump_kin + gamma_gas / ((gamma_gas - 1.0) * prandtl) * jump_temp,
    ]
    values = []
    for component in range(5):
        values.append(
            0.5 * (flux_left[component] + flux_right[component])
            - 0.5 * dissipation[component]
            - viscosity * viscous_terms[component]
        )
    return jnp.stack(values, axis=0)


def flux_change(padded, along, normal):
    length = padded.shape[along]
    face_values = face_flux(
        lax.slice_in_dim(padded, 0, length - 1, axis=along),
        lax.slice_in_dim(padded, 1, length, axis=along),
        normal,
    )
    return lax.slice_in_dim(face_values, 1, length - 1, axis=along) - lax.slice_in_dim(
        face_values, 0, length - 2, axis=along
    )


def spectral_entry(offset, number):
    wrapped = jnp.mod(offset, number)
    parity = 1.0 - 2.0 * jnp.mod(wrapped, 2).astype(jnp.float32)
    angles = math.pi * wrapped.astype(jnp.float32) / number
    sine_val = jnp.where(wrapped == 0, 1.0, jnp.sin(angles))
    derivative = jnp.where(
        wrapped == 0, 0.0, math.pi / number * parity * jnp.cos(angles) / sine_val
    )
    return derivative + 0.5 * parity


def on_device(flow_state, period_match):
    instances = lax.axis_size("inst")
    phase_lag = instances // 4
    instance = lax.axis_index("inst")
    space_parts = lax.axis_size("space")
    position = lax.axis_index("space")
    labels = jnp.arange(period_match.shape[0], dtype=jnp.int32)
    matches = (period_match[:, None] == labels[None, :]).astype(jnp.int32)
    inverse = jnp.sum(labels[:, None] * matches, axis=0)
    mirror = jnp.array([1.0, 1.0, 1.0, -1.0, 1.0], jnp.float32).reshape(5, 1, 1, 1)

    def lagged(plane, steps):
        return from_behind(plane, "inst", steps)

    def timewise(conserved_vars):
        pieces = lax.all_gather(conserved_vars[None], "inst", axis=0, tiled=True)
        number = pieces.shape[0]
        others = jnp.arange(number, dtype=jnp.int32)
        weights = spectral_entry(instance - others, instances)
        return jnp.tensordot(weights, pieces, axes=1, precision=lax.Precision.HIGHEST)

    def evaluate(conserved_vars):
        prims = primitive(conserved_vars)
        padded = extended(prims, (("space", 1),), 1)
        lower_edge = jnp.where(position == 0, prims[:, :1], padded[:, :1])
        upper_edge = jnp.where(position == space_parts - 1, prims[:, -1:], padded[:, -1:])
        along_axial = jnp.concatenate([lower_edge, prims, upper_edge], axis=1)
        along_span = jnp.concatenate(
            [prims[:, :, :1] * mirror, prims, prims[:, :, -1:] * mirror], axis=2
        )
        ghost_below = jnp.take(lagged(prims[..., -1], phase_lag), period_match, axis=2)
        ghost_above = jnp.take(lagged(prims[..., 0], -phase_lag), inverse, axis=2)
        along_pitch = jnp.concatenate(
            [ghost_below[..., None], prims, ghost_above[..., None]], axis=3
        )
        spatial = (
            flux_change(along_axial, 1, 0)
            + flux_change(along_span, 2, 2)
            + flux_change(along_pitch, 3, 1)
        )
        return timewise(conserved_vars) + spatial

    initial = conserved(from_draw(flow_state[0]))
    section_state = initial - pseudo_step * evaluate(initial)
    return evaluate(section_state)[None]


def solution(mesh):
    in_specs = (P(("groups", "inst"), None, "space", None, None), P())
    out_specs = P(("groups", "inst"), None, "space", None, None)
    return jax.shard_map(
        on_device, mesh=mesh, in_specs=in_specs, out_specs=out_specs, check_vma=False
    )
```

profile of v0, /device:TPU:1, one launch (start us, length us, event | category | flops | bytes accessed | tf_op | source)
XLA Modules:
  0.0 72.5 jit_solution(7410314620236597218)
XLA Ops:
  0.0 0.7 copy-done.1
  0.7 1.0 %fusion.15 = f32[5,4,16,128]{3,2,1,0:T(8,128)S(1)} fusion(f32[1,5,4,16,128]{4,3,2,1,0:T(8,128)} %param.7, f32[5]{0:T(128)S(1)} %copy-done.1, f32[5]{0:T(128)S(1)} %copy-done.2), kind=kLoop, calls=%fused_computation.59 | loop fusion | flops 81920 | bytes 327720 | tf_op jit(solution)/shard_map/add | solution.py:41
  1.9 0.5 copy.46
  2.4 2.2 %collective-permute-start.2 = (f32[5,4,16]{0,1,2:T(4,128)S(1)}, f32[5,4,16]{0,1,2:T(4,128)S(1)}, u32[]{:S(2)}, u32[]{:S(2)}) collective-permute-start(f32[5,4,16]{0,1,2:T(4,128)S(1)} %bitcast.389), channel_id=1, source_target_pairs={{12,0},{0,4},{4,8},{8,12},{13,1},{1,5},{5,9},{9,13},{14,2},{2,6},{... | collective-permute-start | bytes 3848 | tf_op jit(solution)/shard_map/ppermute | solution.py:17
  4.5 0.5 copy.49
  5.0 2.1 %collective-permute-start.3 = (f32[5,4,16]{0,1,2:T(4,128)S(1)}, f32[5,4,16]{0,1,2:T(4,128)S(1)}, u32[]{:S(2)}, u32[]{:S(2)}) collective-permute-start(f32[5,4,16]{0,1,2:T(4,128)S(1)} %bitcast.388), channel_id=1, source_target_pairs={{4,0},{8,4},{12,8},{0,12},{5,1},{9,5},{13,9},{1,13},{6,2},{10,6},{... | collective-permute-start | bytes 3848 | tf_op jit(solution)/shard_map/ppermute | solution.py:17
  7.1 4.2 %collective-permute-start = (f32[5,1,16,128]{3,2,1,0:T(8,128)S(1)}, f32[5,1,16,128]{3,2,1,0:T(8,128)S(1)}, u32[]{:S(2)}, u32[]{:S(2)}) collective-permute-start(f32[5,1,16,128]{3,2,1,0:T(8,128)S(1)} %get-tuple-element.119), channel_id=1, source_target_pairs={{0,1},{1,2},{2,3},{4,5},{5,6},{6,7},{8,9},{9,10},{10,11},{12,13},{... | collective-permute-start | bytes 122888 | tf_op jit(solution)/shard_map/ppermute | solution.py:28
  11.3 1.9 %collective-permute-start.1 = (f32[5,1,16,128]{3,2,1,0:T(8,128)S(1)}, f32[5,1,16,128]{3,2,1,0:T(8,128)S(1)}, u32[]{:S(2)}, u32[]{:S(2)}) collective-permute-start(f32[5,1,16,128]{3,2,1,0:T(8,128)S(1)} %get-tuple-element.120), channel_id=1, source_target_pairs={{1,0},{2,1},{3,2},{5,4},{6,5},{7,6},{9,8},{10,9},{11,10},{13,12},{... | collective-permute-start | bytes 122888 | tf_op jit(solution)/shard_map/ppermute | solution.py:30
  13.4 13.8 %all-gather = f32[20,4,16,128]{3,2,1,0:T(8,128)S(1)} all-gather(f32[5,4,16,128]{3,2,1,0:T(8,128)S(1)} %get-tuple-element.130), channel_id=2, replica_groups=mesh['groups'=2,'inst'=4,'space'=4] {'inst'}, dimensions={0}, use_global_device_ids=true | all-gather | bytes 819200 | tf_op jit(solution)/shard_map/all_gather | solution.py:183
  27.2 0.6 copy-done
  28.6 1.5 %fusion.2 = f32[1,5,4,16,128]{4,0,3,2,1:T(1,128)S(1)} fusion(f32[4,5,4,16,128]{4,3,2,1,0:T(8,128)S(1)} %bitcast.384, s32[]{:T(128)S(6)} %axis_index.23), kind=kOutput, calls=%fused_computation.6 | convolution fusion | flops 1966224 | bytes 819204 | tf_op jit(solution)/shard_map/dot_general | solution.py:187
  30.3 0.6 gather_fusion
  31.0 0.6 copy.31
  31.6 0.6 gather_fusion.1
  32.3 0.6 copy.34
  32.8 0.2 maximum_maximum_fusion
  33.2 0.2 subtract_dynamic-update-slice_fusion.3
  33.8 0.2 fusion.61
  34.9 14.5 %all-gather.1 = f32[20,4,16,128]{3,2,1,0:T(8,128)S(1)} all-gather(f32[5,4,16,128]{3,2,1,0:T(8,128)S(1)} %fusion.13), channel_id=3, replica_groups=mesh['groups'=2,'inst'=4,'space'=4] {'inst'}, dimensions={0}, use_global_device_ids=true | all-gather | bytes 819200 | tf_op jit(solution)/shard_map/all_gather | solution.py:183
  49.6 1.5 %fusion = f32[1,5,4,16,128]{4,0,3,2,1:T(1,128)S(1)} fusion(f32[4,5,4,16,128]{4,3,2,1,0:T(8,128)S(1)} %bitcast.385, s32[]{:T(128)S(6)} %axis_index.23), kind=kOutput, calls=%fused_computation.4 | convolution fusion | flops 1966224 | bytes 819204 | tf_op jit(solution)/shard_map/dot_general | solution.py:187
  51.2 0.5 copy.52
  51.7 0.5 copy.53
  52.2 3.3 %collective-permute-start.7 = (f32[5,4,16]{0,1,2:T(4,128)S(1)}, f32[5,4,16]{0,1,2:T(4,128)S(1)}, u32[]{:S(2)}, u32[]{:S(2)}) collective-permute-start(f32[5,4,16]{0,1,2:T(4,128)S(1)} %bitcast.390), channel_id=1, source_target_pairs={{4,0},{8,4},{12,8},{0,12},{5,1},{9,5},{13,9},{1,13},{6,2},{10,6},{... | collective-permute-start | bytes 3848 | tf_op jit(solution)/shard_map/ppermute | solution.py:17
  56.1 8.9 %collective-permute-start.4 = (f32[5,1,16,128]{3,2,1,0:T(8,128)S(1)}, f32[5,1,16,128]{3,2,1,0:T(8,128)S(1)}, u32[]{:S(2)}, u32[]{:S(2)}) collective-permute-start(f32[5,1,16,128]{3,2,1,0:T(8,128)S(1)} %get-tuple-element.105), channel_id=1, source_target_pairs={{0,1},{1,2},{2,3},{4,5},{5,6},{6,7},{8,9},{9,10},{10,11},{12,13},{... | collective-permute-start | bytes 122888 | tf_op jit(solution)/shard_map/ppermute | solution.py:28
  65.0 2.1 %collective-permute-start.5 = (f32[5,1,16,128]{3,2,1,0:T(8,128)S(1)}, f32[5,1,16,128]{3,2,1,0:T(8,128)S(1)}, u32[]{:S(2)}, u32[]{:S(2)}) collective-permute-start(f32[5,1,16,128]{3,2,1,0:T(8,128)S(1)} %get-tuple-element.106), channel_id=1, source_target_pairs={{1,0},{2,1},{3,2},{5,4},{6,5},{7,6},{9,8},{10,9},{11,10},{13,12},{... | collective-permute-start | bytes 122888 | tf_op jit(solution)/shard_map/ppermute | solution.py:30
  67.3 0.6 gather_fusion.2
  68.0 0.6 copy.36
  68.5 0.6 gather_fusion.3
  69.2 0.6 copy.39
  70.1 0.2 subtract_dynamic-update-slice_fusion.1
  70.8 0.2 fusion.50
  71.7 0.8 %fusion.8 = f32[1,5,4,16,128]{4,3,2,1,0:T(8,128)} fusion(f32[5,4,16,128]{3,2,1,0:T(8,128)S(1)} %bitcast.386, f32[5,4,16,129]{3,2,1,0:T(8,128)S(1)} %fusion.50, f32[5,4,17,128]{3,2,1,0:T(8,128)S(1)} %constant_dynamic-update-slice_fusion.15, f32[5,5,16,128]{3,2,1,0:T(8,128)S(1)} %constant_dynamic-update-slice_fusion.10), kind=kLoop, calls=%fused_computation.45 | loop fusion | flops 245760 | bytes 1310720 | tf_op jit(solution)/shard_map/broadcast_in_dim | solution.py:212
  (86 shorter events, 5.4 us)
Async XLA Ops:
  0.0 0.7 copy-start.1
  0.0 0.7 copy-start.2
  2.4 27.9 %collective-permute-start.2 = (f32[5,4,16]{0,1,2:T(4,128)S(1)}, f32[5,4,16]{0,1,2:T(4,128)S(1)}, u32[]{:S(2)}, u32[]{:S(2)}) collective-permute-start(f32[5,4,16]{0,1,2:T(4,128)S(1)} %bitcast.389), channel_id=1, source_target_pairs={{12,0},{0,4},{4,8},{8,12},{13,1},{1,5},{5,9},{9,13},{14,2},{2,6},{... | collective-permute-start | bytes 3848 | tf_op jit(solution)/shard_map/ppermute | solution.py:17
  5.0 26.5 %collective-permute-start.3 = (f32[5,4,16]{0,1,2:T(4,128)S(1)}, f32[5,4,16]{0,1,2:T(4,128)S(1)}, u32[]{:S(2)}, u32[]{:S(2)}) collective-permute-start(f32[5,4,16]{0,1,2:T(4,128)S(1)} %bitcast.388), channel_id=1, source_target_pairs={{4,0},{8,4},{12,8},{0,12},{5,1},{9,5},{13,9},{1,13},{6,2},{10,6},{... | collective-permute-start | bytes 3848 | tf_op jit(solution)/shard_map/ppermute | solution.py:17
  7.1 26.9 %collective-permute-start = (f32[5,1,16,128]{3,2,1,0:T(8,128)S(1)}, f32[5,1,16,128]{3,2,1,0:T(8,128)S(1)}, u32[]{:S(2)}, u32[]{:S(2)}) collective-permute-start(f32[5,1,16,128]{3,2,1,0:T(8,128)S(1)} %get-tuple-element.119), channel_id=1, source_target_pairs={{0,1},{1,2},{2,3},{4,5},{5,6},{6,7},{8,9},{9,10},{10,11},{12,13},{... | collective-permute-start | bytes 122888 | tf_op jit(solution)/shard_map/ppermute | solution.py:28
  11.3 1.9 %copy-start.3 = (s32[16]{0:T(128)S(1)}, s32[16]{0:T(128)}, u32[]{:S(2)}) copy-start(s32[16]{0:T(128)} %param.8) | copy-start | bytes 196
  11.3 22.7 %collective-permute-start.1 = (f32[5,1,16,128]{3,2,1,0:T(8,128)S(1)}, f32[5,1,16,128]{3,2,1,0:T(8,128)S(1)}, u32[]{:S(2)}, u32[]{:S(2)}) collective-permute-start(f32[5,1,16,128]{3,2,1,0:T(8,128)S(1)} %get-tuple-element.120), channel_id=1, source_target_pairs={{1,0},{2,1},{3,2},{5,4},{6,5},{7,6},{9,8},{10,9},{11,10},{13,12},{... | collective-permute-start | bytes 122888 | tf_op jit(solution)/shard_map/ppermute | solution.py:30
  27.2 0.7 copy-start
  51.7 15.6 %collective-permute-start.6 = (f32[5,4,16]{0,1,2:T(4,128)S(1)}, f32[5,4,16]{0,1,2:T(4,128)S(1)}, u32[]{:S(2)}, u32[]{:S(2)}) collective-permute-start(f32[5,4,16]{0,1,2:T(4,128)S(1)} %bitcast.391), channel_id=1, source_target_pairs={{12,0},{0,4},{4,8},{8,12},{13,1},{1,5},{5,9},{9,13},{14,2},{2,6},{... | collective-permute-start | bytes 3848 | tf_op jit(solution)/shard_map/ppermute | solution.py:17
  52.2 16.3 %collective-permute-start.7 = (f32[5,4,16]{0,1,2:T(4,128)S(1)}, f32[5,4,16]{0,1,2:T(4,128)S(1)}, u32[]{:S(2)}, u32[]{:S(2)}) collective-permute-start(f32[5,4,16]{0,1,2:T(4,128)S(1)} %bitcast.390), channel_id=1, source_target_pairs={{4,0},{8,4},{12,8},{0,12},{5,1},{9,5},{13,9},{1,13},{6,2},{10,6},{... | collective-permute-start | bytes 3848 | tf_op jit(solution)/shard_map/ppermute | solution.py:17
  56.1 14.8 %collective-permute-start.4 = (f32[5,1,16,128]{3,2,1,0:T(8,128)S(1)}, f32[5,1,16,128]{3,2,1,0:T(8,128)S(1)}, u32[]{:S(2)}, u32[]{:S(2)}) collective-permute-start(f32[5,1,16,128]{3,2,1,0:T(8,128)S(1)} %get-tuple-element.105), channel_id=1, source_target_pairs={{0,1},{1,2},{2,3},{4,5},{5,6},{6,7},{8,9},{9,10},{10,11},{12,13},{... | collective-permute-start | bytes 122888 | tf_op jit(solution)/shard_map/ppermute | solution.py:28
  65.0 5.9 %collective-permute-start.5 = (f32[5,1,16,128]{3,2,1,0:T(8,128)S(1)}, f32[5,1,16,128]{3,2,1,0:T(8,128)S(1)}, u32[]{:S(2)}, u32[]{:S(2)}) collective-permute-start(f32[5,1,16,128]{3,2,1,0:T(8,128)S(1)} %get-tuple-element.106), channel_id=1, source_target_pairs={{1,0},{2,1},{3,2},{5,4},{6,5},{7,6},{9,8},{10,9},{11,10},{13,12},{... | collective-permute-start | bytes 122888 | tf_op jit(solution)/shard_map/ppermute | solution.py:30
where the time goes:
time: 72.7 us; the launch traced here: 72.5 us
  blocking collectives  28.3 us (39%)
  starting transfers between devices  24.6 us (34%)
  local copies, waits for them, and re-layouts  8.14 us (11%)
  other arithmetic  7.8 us (11%)
  matrix products  3.1 us (4%)
    all_gather x2, blocking collectives, timewise(): pieces = lax.all_gather(conserved_vars[None], 'inst', axis=0, tiled=True)  28.3 us
    ppermute x2, starting transfers between devices, extended(): lax.ppermute(tail, axis, [(i, (i + 1) % count) for i in range(ends)])  13 us
    ppermute x4, starting transfers between devices, from_behind(): return lax.ppermute(block, axis, route)  7.53 us
    ppermute x2, starting transfers between devices, extended(): lax.ppermute(head, axis, [((i + 1) % count, i) for i in range(ends)])  4.02 us
    dot_general x2, matrix products, timewise(): jnp.tensordot(weights, pieces, axes=1, precision=lax.Precision.HIGHEST)  3.1 us
    unnamed x24, other arithmetic  3.02 us
  transfers between devices with their start and end apart: 8, of which 0 were waited for; matrix products, arithmetic and copies ran while one was open for 16% of the time, Pallas kernels for 0%

commit v1 on v0

--- a/solution.py
+++ b/solution.py
@@ -9,6 +9,18 @@
 viscosity = 0.1
 pseudo_step = 0.03
 entropy_share = 0.1
+
+
+def gather_by_bits(x, axis, dim):
+    ways, here = (lax.axis_size(axis), lax.axis_index(axis))
+    grown, reach = (x, 1)
+    while reach < ways:
+        theirs = lax.ppermute(grown, axis, [(d, d ^ reach) for d in range(ways)])
+        mine_first = jnp.concatenate([grown, theirs], axis=dim)
+        theirs_first = jnp.concatenate([theirs, grown], axis=dim)
+        grown = jnp.where(here & reach == 0, mine_first, theirs_first)
+        reach = 2 * reach
+    return grown
 
 
 def from_behind(block, axis, distance):
@@ -180,7 +192,7 @@
         return from_behind(plane, "inst", steps)
 
     def timewise(conserved_vars):
-        pieces = lax.all_gather(conserved_vars[None], "inst", axis=0, tiled=True)
+        pieces = gather_by_bits(conserved_vars[None], "inst", 0)
         number = pieces.shape[0]
         others = jnp.arange(number, dtype=jnp.int32)
         weights = spectral_entry(instance - others, instances)

time: 72.7 us -> 71.8 us (0.988)
  blocking collectives: 28.3 us -> 0 us
  waiting for transfers between devices: 0.02 us -> 28 us
  starting transfers between devices: 24.6 us -> 23.3 us
    all_gather x2 -> x0, blocking collectives: 28.3 us -> none  [timewise(): pieces = lax.all_gather(conserved_vars[None], 'inst', axis=0, tiled=True)]
    ppermute x0 -> x4, waiting for transfers between devices: none -> 28 us  [gather_by_bits(): theirs = lax.ppermute(grown, axis, [(d, d ^ reach) for d in range(ways)])]
    ppermute x2, starting transfers between devices: 13 us -> 9.36 us  [extended(): lax.ppermute(tail, axis, [(i, (i + 1) % count) for i in range(ends)])]
    ppermute x0 -> x4, starting transfers between devices: none -> 3.26 us  [gather_by_bits(): theirs = lax.ppermute(grown, axis, [(d, d ^ reach) for d in range(ways)])]
    ppermute x4, starting transfers between devices: 7.53 us -> 6.63 us  [from_behind(): return lax.ppermute(block, axis, route)]
  transfers between devices with their start and end apart: 8 -> 12, of which waited for: 0 -> 2; matrix products, arithmetic and copies ran while one was open for 16% -> 17% of each run, Pallas kernels for 0% -> 0%
where the time goes in v1:
time: 71.8 us; the launch traced here: 71.1 us
  waiting for transfers between devices  28 us (39%)
  starting transfers between devices  23.3 us (32%)
  local copies, waits for them, and re-layouts  8.13 us (11%)
  other arithmetic  7.95 us (11%)
  matrix products  3.1 us (4%)
    ppermute x4, waiting for transfers between devices, gather_by_bits(): theirs = lax.ppermute(grown, axis, [(d, d ^ reach) for d in range(ways)])  28 us
    ppermute x2, starting transfers between devices, extended(): lax.ppermute(tail, axis, [(i, (i + 1) % count) for i in range(ends)])  9.36 us
    ppermute x4, starting transfers between devices, from_behind(): return lax.ppermute(block, axis, route)  6.63 us
    ppermute x2, starting transfers between devices, extended(): lax.ppermute(head, axis, [((i + 1) % count, i) for i in range(ends)])  4.02 us
    ppermute x4, starting transfers between devices, gather_by_bits(): theirs = lax.ppermute(grown, axis, [(d, d ^ reach) for d in range(ways)])  3.26 us
    dot_general x2, matrix products, timewise(): jnp.tensordot(weights, pieces, axes=1, precision=lax.Precision.HIGHEST)  3.1 us
    unnamed x24, other arithmetic  3.01 us
  transfers between devices with their start and end apart: 12, of which 2 were waited for; matrix products, arithmetic and copies ran while one was open for 17% of the time, Pallas kernels for 0%

profile of v1, /device:TPU:1, one launch (start us, length us, event | category | flops | bytes accessed | tf_op | source)
XLA Modules:
  0.0 71.1 jit_solution(3973791252100116838)
XLA Ops:
  0.0 0.7 copy-done.1
  0.7 1.0 %fusion.15 = f32[5,4,16,128]{3,2,1,0:T(8,128)S(1)} fusion(f32[1,5,4,16,128]{4,3,2,1,0:T(8,128)} %param.7, f32[5]{0:T(128)S(1)} %copy-done.1, f32[5]{0:T(128)S(1)} %copy-done.2), kind=kLoop, calls=%fused_computation.63 | loop fusion | flops 81920 | bytes 327720 | tf_op jit(solution)/shard_map/add | solution.py:53
  1.8 2.2 %collective-permute-start = (f32[1,5,4,16,128]{4,3,2,1,0:T(8,128)S(1)}, f32[1,5,4,16,128]{4,3,2,1,0:T(8,128)S(1)}, u32[]{:S(2)}, u32[]{:S(2)}) collective-permute-start(f32[1,5,4,16,128]{4,3,2,1,0:T(8,128)S(1)} %get-tuple-element.131), channel_id=1, source_target_pairs={{0,4},{4,0},{8,12},{12,8},{1,5},{5,1},{9,13},{13,9},{2,6},{6,2},{1... | collective-permute-start | bytes 491528 | tf_op jit(solution)/shard_map/ppermute | solution.py:18
  4.1 0.5 copy.35
  4.6 0.5 copy.38
  5.1 3.3 %collective-permute-start.5 = (f32[5,4,16]{0,1,2:T(4,128)S(1)}, f32[5,4,16]{0,1,2:T(4,128)S(1)}, u32[]{:S(2)}, u32[]{:S(2)}) collective-permute-start(f32[5,4,16]{0,1,2:T(4,128)S(1)} %bitcast.389), channel_id=1, source_target_pairs={{4,0},{8,4},{12,8},{0,12},{5,1},{9,5},{13,9},{1,13},{6,2},{10,6},{... | collective-permute-start | bytes 3848 | tf_op jit(solution)/shard_map/ppermute | solution.py:29
  8.4 4.5 %collective-permute-start.2 = (f32[5,1,16,128]{3,2,1,0:T(8,128)S(1)}, f32[5,1,16,128]{3,2,1,0:T(8,128)S(1)}, u32[]{:S(2)}, u32[]{:S(2)}) collective-permute-start(f32[5,1,16,128]{3,2,1,0:T(8,128)S(1)} %get-tuple-element.119), channel_id=1, source_target_pairs={{0,1},{1,2},{2,3},{4,5},{5,6},{6,7},{8,9},{9,10},{10,11},{12,13},{... | collective-permute-start | bytes 122888 | tf_op jit(solution)/shard_map/ppermute | solution.py:40
  12.9 1.9 %collective-permute-start.3 = (f32[5,1,16,128]{3,2,1,0:T(8,128)S(1)}, f32[5,1,16,128]{3,2,1,0:T(8,128)S(1)}, u32[]{:S(2)}, u32[]{:S(2)}) collective-permute-start(f32[5,1,16,128]{3,2,1,0:T(8,128)S(1)} %get-tuple-element.120), channel_id=1, source_target_pairs={{1,0},{2,1},{3,2},{5,4},{6,5},{7,6},{9,8},{10,9},{11,10},{13,12},{... | collective-permute-start | bytes 122888 | tf_op jit(solution)/shard_map/ppermute | solution.py:42
  15.0 0.6 copy-done
  16.6 0.6 gather_fusion
  17.3 0.6 copy.20
  17.8 0.6 gather_fusion.1
  18.5 0.6 copy.23
  19.4 0.2 subtract_dynamic-update-slice_fusion.3
  20.8 0.6 collective-permute-start.1
  21.6 13.7 %collective-permute-done.1 = f32[2,5,4,16,128]{4,3,2,1,0:T(8,128)S(1)} collective-permute-done((f32[2,5,4,16,128]{4,3,2,1,0:T(8,128)S(1)}, f32[2,5,4,16,128]{4,3,2,1,0:T(8,128)S(1)}, u32[]{:S(2)}, u32[]{:S(2)}) %collective-permute-start.1) | collective-permute-done | bytes 327712 | tf_op jit(solution)/shard_map/ppermute | solution.py:18
  35.4 1.5 %fusion.2 = f32[1,5,4,16,128]{4,0,3,2,1:T(1,128)S(1)} fusion(f32[4,5,4,16,128]{4,3,2,1,0:T(8,128)S(1)} %maximum_select_fusion, s32[]{:T(128)S(6)} %axis_index.15), kind=kOutput, calls=%fused_computation.8 | convolution fusion | flops 1966224 | bytes 819204 | tf_op jit(solution)/shard_map/dot_general | solution.py:199
  37.5 0.5 copy.41
  38.0 1.5 %collective-permute-start.10 = (f32[5,4,16]{0,1,2:T(4,128)S(1)}, f32[5,4,16]{0,1,2:T(4,128)S(1)}, u32[]{:S(2)}, u32[]{:S(2)}) collective-permute-start(f32[5,4,16]{0,1,2:T(4,128)S(1)} %bitcast.392), channel_id=1, source_target_pairs={{12,0},{0,4},{4,8},{8,12},{13,1},{1,5},{5,9},{9,13},{14,2},{2,6},{... | collective-permute-start | bytes 3848 | tf_op jit(solution)/shard_map/ppermute | solution.py:29
  39.4 0.5 copy.42
  39.9 1.8 %collective-permute-start.11 = (f32[5,4,16]{0,1,2:T(4,128)S(1)}, f32[5,4,16]{0,1,2:T(4,128)S(1)}, u32[]{:S(2)}, u32[]{:S(2)}) collective-permute-start(f32[5,4,16]{0,1,2:T(4,128)S(1)} %bitcast.391), channel_id=1, source_target_pairs={{4,0},{8,4},{12,8},{0,12},{5,1},{9,5},{13,9},{1,13},{6,2},{10,6},{... | collective-permute-start | bytes 3848 | tf_op jit(solution)/shard_map/ppermute | solution.py:29
  42.4 4.8 %collective-permute-start.8 = (f32[5,1,16,128]{3,2,1,0:T(8,128)S(1)}, f32[5,1,16,128]{3,2,1,0:T(8,128)S(1)}, u32[]{:S(2)}, u32[]{:S(2)}) collective-permute-start(f32[5,1,16,128]{3,2,1,0:T(8,128)S(1)} %get-tuple-element.105), channel_id=1, source_target_pairs={{0,1},{1,2},{2,3},{4,5},{5,6},{6,7},{8,9},{9,10},{10,11},{12,13},{... | collective-permute-start | bytes 122888 | tf_op jit(solution)/shard_map/ppermute | solution.py:40
  47.3 2.1 %collective-permute-start.9 = (f32[5,1,16,128]{3,2,1,0:T(8,128)S(1)}, f32[5,1,16,128]{3,2,1,0:T(8,128)S(1)}, u32[]{:S(2)}, u32[]{:S(2)}) collective-permute-start(f32[5,1,16,128]{3,2,1,0:T(8,128)S(1)} %get-tuple-element.106), channel_id=1, source_target_pairs={{1,0},{2,1},{3,2},{5,4},{6,5},{7,6},{9,8},{10,9},{11,10},{13,12},{... | collective-permute-start | bytes 122888 | tf_op jit(solution)/shard_map/ppermute | solution.py:42
  49.5 0.6 gather_fusion.2
  50.2 0.6 copy.25
  50.8 0.6 gather_fusion.3
  51.5 0.6 copy.28
  52.4 0.2 subtract_dynamic-update-slice_fusion.1
  53.8 0.4 collective-permute-start.7
  54.4 14.2 %collective-permute-done.7 = f32[2,5,4,16,128]{4,3,2,1,0:T(8,128)S(1)} collective-permute-done((f32[2,5,4,16,128]{4,3,2,1,0:T(8,128)S(1)}, f32[2,5,4,16,128]{4,3,2,1,0:T(8,128)S(1)}, u32[]{:S(2)}, u32[]{:S(2)}) %collective-permute-start.7) | collective-permute-done | bytes 327712 | tf_op jit(solution)/shard_map/ppermute | solution.py:18
  68.7 1.5 %fusion = f32[1,5,4,16,128]{4,0,3,2,1:T(1,128)S(1)} fusion(f32[4,5,4,16,128]{4,3,2,1,0:T(8,128)S(1)} %maximum_select_fusion.1, s32[]{:T(128)S(6)} %axis_index.15), kind=kOutput, calls=%fused_computation.6 | convolution fusion | flops 1966224 | bytes 819204 | tf_op jit(solution)/shard_map/dot_general | solution.py:199
  70.3 0.8 %fusion.8 = f32[1,5,4,16,128]{4,3,2,1,0:T(8,128)} fusion(f32[5,4,16,128]{3,2,1,0:T(8,128)S(1)} %bitcast.387, f32[5,4,16,129]{3,2,1,0:T(8,128)S(1)} %fusion.51, f32[5,4,17,128]{3,2,1,0:T(8,128)S(1)} %constant_dynamic-update-slice_fusion.15, f32[5,5,16,128]{3,2,1,0:T(8,128)S(1)} %constant_dynamic-update-slice_fusion.10), kind=kLoop, calls=%fused_computation.49 | loop fusion | flops 245760 | bytes 1310720 | tf_op jit(solution)/shard_map/broadcast_in_dim | solution.py:224
  (96 shorter events, 6.1 us)
Async XLA Ops:
  0.0 0.7 copy-start.1
  0.0 0.7 copy-start.2
  1.8 19.0 %collective-permute-start = (f32[1,5,4,16,128]{4,3,2,1,0:T(8,128)S(1)}, f32[1,5,4,16,128]{4,3,2,1,0:T(8,128)S(1)}, u32[]{:S(2)}, u32[]{:S(2)}) collective-permute-start(f32[1,5,4,16,128]{4,3,2,1,0:T(8,128)S(1)} %get-tuple-element.131), channel_id=1, source_target_pairs={{0,4},{4,0},{8,12},{12,8},{1,5},{5,1},{9,13},{13,9},{2,6},{6,2},{1... | collective-permute-start | bytes 491528 | tf_op jit(solution)/shard_map/ppermute | solution.py:18
  4.6 12.0 %collective-permute-start.4 = (f32[5,4,16]{0,1,2:T(4,128)S(1)}, f32[5,4,16]{0,1,2:T(4,128)S(1)}, u32[]{:S(2)}, u32[]{:S(2)}) collective-permute-start(f32[5,4,16]{0,1,2:T(4,128)S(1)} %bitcast.390), channel_id=1, source_target_pairs={{12,0},{0,4},{4,8},{8,12},{13,1},{1,5},{5,9},{9,13},{14,2},{2,6},{... | collective-permute-start | bytes 3848 | tf_op jit(solution)/shard_map/ppermute | solution.py:29
  5.1 12.7 %collective-permute-start.5 = (f32[5,4,16]{0,1,2:T(4,128)S(1)}, f32[5,4,16]{0,1,2:T(4,128)S(1)}, u32[]{:S(2)}, u32[]{:S(2)}) collective-permute-start(f32[5,4,16]{0,1,2:T(4,128)S(1)} %bitcast.389), channel_id=1, source_target_pairs={{4,0},{8,4},{12,8},{0,12},{5,1},{9,5},{13,9},{1,13},{6,2},{10,6},{... | collective-permute-start | bytes 3848 | tf_op jit(solution)/shard_map/ppermute | solution.py:29
  8.4 6.5 %copy-start.3 = (s32[16]{0:T(128)S(1)}, s32[16]{0:T(128)}, u32[]{:S(2)}) copy-start(s32[16]{0:T(128)} %param.8) | copy-start | bytes 196
  8.4 11.9 %collective-permute-start.2 = (f32[5,1,16,128]{3,2,1,0:T(8,128)S(1)}, f32[5,1,16,128]{3,2,1,0:T(8,128)S(1)}, u32[]{:S(2)}, u32[]{:S(2)}) collective-permute-start(f32[5,1,16,128]{3,2,1,0:T(8,128)S(1)} %get-tuple-element.119), channel_id=1, source_target_pairs={{0,1},{1,2},{2,3},{4,5},{5,6},{6,7},{8,9},{9,10},{10,11},{12,13},{... | collective-permute-start | bytes 122888 | tf_op jit(solution)/shard_map/ppermute | solution.py:40
  12.9 7.3 %collective-permute-start.3 = (f32[5,1,16,128]{3,2,1,0:T(8,128)S(1)}, f32[5,1,16,128]{3,2,1,0:T(8,128)S(1)}, u32[]{:S(2)}, u32[]{:S(2)}) collective-permute-start(f32[5,1,16,128]{3,2,1,0:T(8,128)S(1)} %get-tuple-element.120), channel_id=1, source_target_pairs={{1,0},{2,1},{3,2},{5,4},{6,5},{7,6},{9,8},{10,9},{11,10},{13,12},{... | collective-permute-start | bytes 122888 | tf_op jit(solution)/shard_map/ppermute | solution.py:42
  15.0 0.7 copy-start
  20.8 14.5 %collective-permute-start.1 = (f32[2,5,4,16,128]{4,3,2,1,0:T(8,128)S(1)}, f32[2,5,4,16,128]{4,3,2,1,0:T(8,128)S(1)}, u32[]{:S(2)}, u32[]{:S(2)}) collective-permute-start(f32[2,5,4,16,128]{4,3,2,1,0:T(8,128)S(1)} %maximum_select_fusion.2), channel_id=1, source_target_pairs={{0,8},{4,12},{8,0},{12,4},{1,9},{5,13},{9,1},{13,5},{2,10},{6,14},... | collective-permute-start | bytes 983048 | tf_op jit(solution)/shard_map/ppermute | solution.py:18
  37.4 16.4 %collective-permute-start.6 = (f32[1,5,4,16,128]{4,3,2,1,0:T(8,128)S(1)}, f32[1,5,4,16,128]{4,3,2,1,0:T(8,128)S(1)}, u32[]{:S(2)}, u32[]{:S(2)}) collective-permute-start(f32[1,5,4,16,128]{4,3,2,1,0:T(8,128)S(1)} %bitcast.385), channel_id=1, source_target_pairs={{0,4},{4,0},{8,12},{12,8},{1,5},{5,1},{9,13},{13,9},{2,6},{6,2},{1... | collective-permute-start | bytes 491528 | tf_op jit(solution)/shard_map/ppermute | solution.py:18
  38.0 11.6 %collective-permute-start.10 = (f32[5,4,16]{0,1,2:T(4,128)S(1)}, f32[5,4,16]{0,1,2:T(4,128)S(1)}, u32[]{:S(2)}, u32[]{:S(2)}) collective-permute-start(f32[5,4,16]{0,1,2:T(4,128)S(1)} %bitcast.392), channel_id=1, source_target_pairs={{12,0},{0,4},{4,8},{8,12},{13,1},{1,5},{5,9},{9,13},{14,2},{2,6},{... | collective-permute-start | bytes 3848 | tf_op jit(solution)/shard_map/ppermute | solution.py:29
  39.9 10.9 %collective-permute-start.11 = (f32[5,4,16]{0,1,2:T(4,128)S(1)}, f32[5,4,16]{0,1,2:T(4,128)S(1)}, u32[]{:S(2)}, u32[]{:S(2)}) collective-permute-start(f32[5,4,16]{0,1,2:T(4,128)S(1)} %bitcast.391), channel_id=1, source_target_pairs={{4,0},{8,4},{12,8},{0,12},{5,1},{9,5},{13,9},{1,13},{6,2},{10,6},{... | collective-permute-start | bytes 3848 | tf_op jit(solution)/shard_map/ppermute | solution.py:29
  42.4 10.8 %collective-permute-start.8 = (f32[5,1,16,128]{3,2,1,0:T(8,128)S(1)}, f32[5,1,16,128]{3,2,1,0:T(8,128)S(1)}, u32[]{:S(2)}, u32[]{:S(2)}) collective-permute-start(f32[5,1,16,128]{3,2,1,0:T(8,128)S(1)} %get-tuple-element.105), channel_id=1, source_target_pairs={{0,1},{1,2},{2,3},{4,5},{5,6},{6,7},{8,9},{9,10},{10,11},{12,13},{... | collective-permute-start | bytes 122888 | tf_op jit(solution)/shard_map/ppermute | solution.py:40
  47.3 6.0 %collective-permute-start.9 = (f32[5,1,16,128]{3,2,1,0:T(8,128)S(1)}, f32[5,1,16,128]{3,2,1,0:T(8,128)S(1)}, u32[]{:S(2)}, u32[]{:S(2)}) collective-permute-start(f32[5,1,16,128]{3,2,1,0:T(8,128)S(1)} %get-tuple-element.106), channel_id=1, source_target_pairs={{1,0},{2,1},{3,2},{5,4},{6,5},{7,6},{9,8},{10,9},{11,10},{13,12},{... | collective-permute-start | bytes 122888 | tf_op jit(solution)/shard_map/ppermute | solution.py:42
  53.8 14.9 %collective-permute-start.7 = (f32[2,5,4,16,128]{4,3,2,1,0:T(8,128)S(1)}, f32[2,5,4,16,128]{4,3,2,1,0:T(8,128)S(1)}, u32[]{:S(2)}, u32[]{:S(2)}) collective-permute-start(f32[2,5,4,16,128]{4,3,2,1,0:T(8,128)S(1)} %maximum_select_fusion.3), channel_id=1, source_target_pairs={{0,8},{4,12},{8,0},{12,4},{1,9},{5,13},{9,1},{13,5},{2,10},{6,14},... | collective-permute-start | bytes 983048 | tf_op jit(solution)/shard_map/ppermute | solution.py:18
